TPU v7x, 32 devices: a whole 2x2x4 slice. The times are simulated.
32 devices in a mesh: tm: 16 (over z, x, core), rows: 2 (over y).
Axes of the slice: x: 2, y: 2, z: 4, core: 2. Of those that a mesh axis runs over, the one named last changes fastest.
Arguments:
- video: bfloat16 [32, 16, 480, 128], P('tm', 'rows'), may hold values from -1000 to 1000, as said below
- spatial_weight: bfloat16 [3, 3, 128, 128], replicated, may hold values from -0.1875 to 0.1875
- norm_gain: float32 [128], replicated, may hold values from 0.5 to 1.5
- norm_shift: float32 [128], replicated, may hold values from -3 to 3
- temporal_weight: bfloat16 [3, 3, 128, 128], replicated, may hold values from -0.3125 to 0.3125
Outputs:
- encoded: bfloat16 [32, 16, 480, 128], P('tm', 'rows')
Inputs may be any that keep to these rules, and one draw needn't show every extreme that they name: `video`: feature values are finite and of moderate size.
All inputs are finite; a program needn't handle non-finite values.
Results may differ from a plain program's by a relative error of at most 0.0065.
Values may be sent and summed in bfloat16 or wider, within the bound.
No kernel may reach another device: no remote copies, remote signals or barrier semaphores. Data moves between devices by JAX's collectives and lax.ppermute only.
A program may use at most 64 MiB of HBM per device.

v0:
```python
import jax
import jax.numpy as jnp
from jax import lax
from jax.sharding import PartitionSpec as P

GROUPS = 32


def padded_2(array, sides, width):
    for axis, dim in sides:
        size, length = (lax.axis_size(axis), array.shape[dim])
        up = [(i, (i + 1) % size) for i in range(size - 1)]
        down = [(j, i) for i, j in up]
        last = lax.slice_in_dim(array, length - width, length, axis=dim)
        leading = lax.slice_in_dim(array, 0, width, axis=dim)
        before = lax.ppermute(last, axis, up)
        after = lax.ppermute(leading, axis, down)
        array = jnp.concatenate([before, array, after], axis=dim)
    return array


def temporal_layer(extended, lead, dilation, kernels):
    own = extended.shape[0] - lead
    total = extended[lead:].astype(jnp.float32)
    for tap_index in range(3):
        start = lead - tap_index * dilation
        total = total + jnp.einsum(
            "trwc,cd->trwd",
            extended[start : start + own],
            kernels[tap_index],
            preferred_element_type=jnp.float32,
        )
    return total.astype(jnp.bfloat16)


def body(video, spatial_weight, norm_gain, norm_shift, temporal_weight):
    fr_local, band, width, chans = video.shape
    padded = padded_2(video, (("rows", 1),), 1)
    padded = jnp.pad(padded, ((0, 0), (0, 0), (1, 1), (0, 0)))
    pieces = [
        padded[:, row_tap : row_tap + band, col_tap : col_tap + width, :]
        for row_tap in range(3)
        for col_tap in range(3)
    ]
    patches = jnp.concatenate(pieces, axis=-1).reshape(fr_local * band * width, 9 * chans)
    conv = jnp.dot(
        patches, spatial_weight.reshape(9 * chans, chans), preferred_element_type=jnp.float32
    )
    per_group = chans // GROUPS
    grouped = conv.reshape(fr_local, band, width, GROUPS, per_group)
    part_sum = jnp.sum(grouped, axis=(1, 2, 4))
    part_square = jnp.sum(grouped * grouped, axis=(1, 2, 4))
    total_sum, total_square = lax.psum((part_sum, part_square), "rows")
    count = jnp.float32(band * lax.axis_size("rows") * width * per_group)
    mean = total_sum / count
    var = total_square / count - mean * mean
    normed = (grouped - mean[:, None, None, :, None]) * lax.rsqrt(var + 1e-05)[
        :, None, None, :, None
    ]
    normed = normed.reshape(fr_local, band, width, chans) * norm_gain + norm_shift
    hidden = jax.nn.silu(normed).astype(jnp.bfloat16)
    current = lax.all_to_all(hidden, "tm", split_axis=2, concat_axis=0, tiled=True)
    for layer, dilation in enumerate((1, 2, 4)):
        lead = 2 * dilation
        extended = jnp.pad(current, ((lead, 0), (0, 0), (0, 0), (0, 0)))
        current = temporal_layer(extended, lead, dilation, temporal_weight[layer])
    return lax.all_to_all(current, "tm", split_axis=0, concat_axis=2, tiled=True)


def solution(mesh):
    return jax.shard_map(
        body,
        mesh=mesh,
        in_specs=(P("tm", "rows", None, None), P(), P(), P(), P()),
        out_specs=P("tm", "rows", None, None),
        check_vma=False,
    )
```

profile of v0, /device:TPU:1, one launch (start us, length us, event | category | flops | bytes accessed | tf_op | source)
XLA Modules:
  0.0 154.6 jit_solution(4578269416225532073)
XLA Ops:
  0.0 1.1 fusion.36
  1.1 4.0 %collective-permute-start = (bf16[2,1,480,128]{3,2,1,0:T(8,128)(2,1)S(1)}, bf16[2,1,480,128]{3,2,1,0:T(8,128)(2,1)S(1)}, u32[]{:S(2)}, u32[]{:S(2)}) collective-permute-start(bf16[2,1,480,128]{3,2,1,0:T(8,128)(2,1)S(1)} %get-tuple-element.9), channel_id=1, source_target_pairs={{0,1},{2,3},{4,5},{6,7},{8,9},{10,11},{12,13},{14,15},{16,17},{18,... | collective-permute-start | bytes 737288 | tf_op jit(solution)/shard_map/ppermute | solution.py:16
  5.1 1.3 collective-permute-start.1
  6.4 1.2 copy.14
  7.7 2.0 %collective-permute-done = bf16[2,1,480,128]{3,2,1,0:T(8,128)(2,1)S(1)} collective-permute-done((bf16[2,1,480,128]{3,2,1,0:T(8,128)(2,1)S(1)}, bf16[2,1,480,128]{3,2,1,0:T(8,128)(2,1)S(1)}, u32[]{:S(2)}, u32[]{:S(2)}) %collective-permute-start) | collective-permute-done | bytes 245792 | tf_op jit(solution)/shard_map/ppermute | solution.py:16
  9.7 3.8 %collective-permute-done.1 = bf16[2,1,480,128]{3,2,1,0:T(8,128)(2,1)S(1)} collective-permute-done((bf16[2,1,480,128]{3,2,1,0:T(8,128)(2,1)S(1)}, bf16[2,1,480,128]{3,2,1,0:T(8,128)(2,1)S(1)}, u32[]{:S(2)}, u32[]{:S(2)}) %collective-permute-start.1) | collective-permute-done | bytes 245792 | tf_op jit(solution)/shard_map/ppermute | solution.py:17
  13.5 2.1 %fusion.7 = bf16[2,10,482,128]{3,2,1,0:T(8,128)(2,1)S(1)} fusion(bf16[2,1,480,128]{3,2,1,0:T(8,128)(2,1)S(1)} %collective-permute-done.1, bf16[2,8,480,128]{3,2,1,0:T(8,128)(2,1)} %param.5, bf16[2,1,480,128]{3,2,1,0:T(8,128)(2,1)S(1)} %collective-permute-done), kind=kLoop, calls=%fused_computation.15 | loop fusion | flops 14807040 | bytes 4925440 | tf_op jit(solution)/shard_map/concatenate | solution.py:18
  16.4 0.8 slice_dynamic-update-slice_fusion.4
  18.2 0.8 slice_dynamic-update-slice_fusion.2
  20.0 0.8 slice_dynamic-update-slice_fusion
  20.8 7.1 %fusion.35 = (f32[2,32]{1,0:T(2,128)S(1)}, f32[2,32]{1,0:T(2,128)S(1)}, f32[2,8,480,32,4]{2,3,4,1,0:T(8,128)}) fusion(bf16[32,4,1152,1,1]{2,1,0,4,3:T(4,128)(2,1)S(1)} %bitcast.100, bf16[2,8,480,1152]{3,2,1,0:T(8,128)(2,1)S(1)} %slice_dynamic-update-slice_fusion), kind=kOutput, calls=%fused_computation.54 | convolution fusion | flops 2267873280 | bytes 21922304 | tf_op jit(solution)/shard_map/dot_general | solution.py:46
  27.9 3.9 %all-reduce.4 = (f32[2,32]{1,0:T(2,128)S(1)}, f32[2,32]{1,0:T(2,128)S(1)}) all-reduce(f32[2,32]{1,0:T(2,128)S(1)} %get-tuple-element.6, f32[2,32]{1,0:T(2,128)S(1)} %get-tuple-element.5), channel_id=1, replica_groups=mesh['tm'=16,'rows'=2] {'rows'}, use_global_device_ids=true, to_apply=%region_3.4 | all-reduce | flops 128 | bytes 1024 | tf_op jit(solution)/shard_map/psum | solution.py:53
  31.8 2.9 %subtract_multiply_fusion = f32[2,8,480,32,4]{2,3,4,1,0:T(8,128)S(1)} fusion(f32[2,8,480,32,4]{2,3,4,1,0:T(8,128)} %get-tuple-element.13, f32[2,32]{1,0:T(2,128)S(1)} %get-tuple-element.12, f32[2,32]{1,0:T(2,128)S(1)} %get-tuple-element.11), kind=kLoop, calls=%fused_computation.7 | loop fusion | flops 1966080 | bytes 7864832 | tf_op jit(solution)/shard_map/mul | solution.py:57
  34.7 2.4 %copy.16 = f32[2,8,480,32,4]{2,1,4,3,0:T(8,128)S(1)} copy(f32[2,8,480,32,4]{2,3,4,1,0:T(8,128)S(1)} %subtract_multiply_fusion) | data formatting | bytes 7864320 | tf_op jit(solution)/shard_map/mul | solution.py:57
  37.2 1.4 multiply_convert_fusion
  38.7 3.4 %copy.17 = bf16[2,8,480,128]{3,1,0,2:T(8,128)(2,1)} copy(bf16[2,8,480,128]{2,1,3,0:T(8,128)(2,1)S(1)} %multiply_convert_fusion) | data formatting | bytes 3932160 | tf_op jit(solution)/shard_map/convert_element_type | solution.py:61
  42.0 54.3 %all_to_all.36 = bf16[2,8,480,128]{3,1,0,2:T(8,128)(2,1)S(1)} all-to-all(bf16[2,8,480,128]{3,1,0,2:T(8,128)(2,1)} %copy.17), channel_id=1, replica_groups=mesh['tm'=16,'rows'=2] {'tm'}, dimensions={2} | all-to-all | bytes 3932160 | tf_op jit(solution)/shard_map/all_to_all | solution.py:62
  98.0 0.9 add_convert_fusion.2
  99.6 0.7 fusion.19
  100.3 1.0 add_convert_fusion.1
  102.0 0.7 fusion.14
  102.6 1.0 add_convert_fusion
  103.6 49.4 %all_to_all.37 = bf16[32,8,30,128]{3,1,2,0:T(8,128)(2,1)S(1)} all-to-all(bf16[32,8,30,128]{3,1,2,0:T(8,128)(2,1)S(1)} %add_convert_fusion), channel_id=1, replica_groups=mesh['tm'=16,'rows'=2] {'tm'}, dimensions={0} | all-to-all | bytes 3932160 | tf_op jit(solution)/shard_map/all_to_all | solution.py:67
  153.1 1.5 copy.21
  (22 shorter events, 5.9 us)
Async XLA Ops:
  1.1 8.6 %collective-permute-start = (bf16[2,1,480,128]{3,2,1,0:T(8,128)(2,1)S(1)}, bf16[2,1,480,128]{3,2,1,0:T(8,128)(2,1)S(1)}, u32[]{:S(2)}, u32[]{:S(2)}) collective-permute-start(bf16[2,1,480,128]{3,2,1,0:T(8,128)(2,1)S(1)} %get-tuple-element.9), channel_id=1, source_target_pairs={{0,1},{2,3},{4,5},{6,7},{8,9},{10,11},{12,13},{14,15},{16,17},{18,... | collective-permute-start | bytes 737288 | tf_op jit(solution)/shard_map/ppermute | solution.py:16
  5.1 8.4 %collective-permute-start.1 = (bf16[2,1,480,128]{3,2,1,0:T(8,128)(2,1)S(1)}, bf16[2,1,480,128]{3,2,1,0:T(8,128)(2,1)S(1)}, u32[]{:S(2)}, u32[]{:S(2)}) collective-permute-start(bf16[2,1,480,128]{3,2,1,0:T(8,128)(2,1)S(1)} %get-tuple-element.10), channel_id=1, source_target_pairs={{1,0},{3,2},{5,4},{7,6},{9,8},{11,10},{13,12},{15,14},{17,16},{19,... | collective-permute-start | bytes 737288 | tf_op jit(solution)/shard_map/ppermute | solution.py:17
  7.6 8.3 %copy-start = (bf16[2,8,480,128]{3,2,1,0:T(8,128)(2,1)S(1)}, bf16[2,8,480,128]{3,2,1,0:T(8,128)(2,1)}, u32[]{:S(2)}) copy-start(bf16[2,8,480,128]{3,2,1,0:T(8,128)(2,1)} %param.5) | copy-start | bytes 5898244
  34.7 2.5 %copy-start.2 = (f32[128]{0:T(128)S(1)}, f32[128]{0:T(128)}, u32[]{:S(2)}) copy-start(f32[128]{0:T(128)} %param.8) | copy-start | bytes 1540
  34.7 2.5 %copy-start.3 = (f32[128]{0:T(128)S(1)}, f32[128]{0:T(128)}, u32[]{:S(2)}) copy-start(f32[128]{0:T(128)} %param.7) | copy-start | bytes 1540
  42.0 54.7 %copy-start.1 = (bf16[3,3,128,128]{3,2,1,0:T(8,128)(2,1)S(1)}, bf16[3,3,128,128]{3,2,1,0:T(8,128)(2,1)}, u32[]{:S(2)}) copy-start(bf16[3,3,128,128]{3,2,1,0:T(8,128)(2,1)} %param.9) | copy-start | bytes 884740
where the time goes:
time: 155 us
  blocking collectives  108 us (70%)
  local copies, waits for them, and re-layouts  14.3 us (9%)
  matrix products  13.9 us (9%)
  other arithmetic  7.38 us (5%)
  waiting for transfers between devices  5.84 us (4%)
  starting transfers between devices  5.28 us (3%)
    all_to_all x1, blocking collectives, body(): lax.all_to_all(hidden, 'tm', split_axis=2, concat_axis=0, tiled=True)  54.3 us
    all_to_all x1, blocking collectives, body(): lax.all_to_all(current, 'tm', split_axis=0, concat_axis=2, tiled=True)  49.4 us
    dot_general x1, matrix products, body(): jnp.dot(patches, spatial_weight.reshape(9 * chans, chans), preferred_elem...  7.06 us
    dot_general x9, matrix products, temporal_layer(): jnp.einsum('trwc,cd->trwd', extended[start:start + own], kernels[tap_inde...  6.82 us
    ppermute x1, starting transfers between devices, padded_2(): before = lax.ppermute(last, axis, up)  3.99 us
    psum x1, blocking collectives, body(): total_sum, total_square = lax.psum((part_sum, part_square), 'rows')  3.95 us
    ppermute x1, waiting for transfers between devices, padded_2(): after = lax.ppermute(leading, axis, down)  3.81 us
    unnamed x14, local copies, waits for them, and re-layouts  3.41 us
  transfers between devices with their start and end apart: 2, of which 2 were waited for; matrix products, arithmetic and copies ran while one was open for 1% of the time, Pallas kernels for 0%

commit v1 on v0

--- a/solution.py
+++ b/solution.py
@@ -4,6 +4,28 @@
 from jax.sharding import PartitionSpec as P
 
 GROUPS = 32
+
+
+def cut_along(x, dim, size):
+    before, after = (x.shape[:dim], x.shape[dim + 1 :])
+    return jnp.moveaxis(x.reshape(*before, size, -1, *after), dim, 0)
+
+
+def in_order(blocks, dim):
+    blocks = jnp.moveaxis(blocks, 0, dim)
+    shape = blocks.shape
+    return blocks.reshape(*shape[:dim], shape[dim] * shape[dim + 1], *shape[dim + 2 :])
+
+
+def exchange_in_pairs(x, axis, split_dim, concat_dim):
+    size, mine = (lax.axis_size(axis), lax.axis_index(axis))
+    pieces = cut_along(x, split_dim, size)
+    outs = [pieces[mine]]
+    for step in range(1, size):
+        sent = pieces[mine ^ step]
+        outs.append(lax.ppermute(sent, axis, [(i, i ^ step) for i in range(size)]))
+    pieces = jnp.stack(outs)[mine ^ jnp.arange(size)]
+    return in_order(pieces, concat_dim)
 
 
 def padded_2(array, sides, width):
@@ -59,7 +81,7 @@
     ]
     normed = normed.reshape(fr_local, band, width, chans) * norm_gain + norm_shift
     hidden = jax.nn.silu(normed).astype(jnp.bfloat16)
-    current = lax.all_to_all(hidden, "tm", split_axis=2, concat_axis=0, tiled=True)
+    current = exchange_in_pairs(hidden, "tm", 2, 0)
     for layer, dilation in enumerate((1, 2, 4)):
         lead = 2 * dilation
         extended = jnp.pad(current, ((lead, 0), (0, 0), (0, 0), (0, 0)))

time: 155 us -> 234 us (1.51)
  local copies, waits for them, and re-layouts: 14.3 us -> 95.9 us
  blocking collectives: 108 us -> 60.7 us
  starting transfers between devices: 5.28 us -> 37.9 us
  other arithmetic: 7.38 us -> 13.4 us
  waiting for transfers between devices: 5.84 us -> 10.6 us
    all_to_all x1 -> x0, blocking collectives: 54.3 us -> none  [body(): lax.all_to_all(hidden, 'tm', split_axis=2, concat_axis=0, tiled=True)]
    another operation x0 -> x18, local copies, waits for them, and re-layouts: none -> 52.2 us
    ppermute x0 -> x15, starting transfers between devices: none -> 32.6 us  [exchange_in_pairs(): outs.append(lax.ppermute(sent, axis, [(i, i ^ step) for i in range(size)]))]
    unnamed x14 -> x41, local copies, waits for them, and re-layouts: 3.41 us -> 17.8 us
    reshape x0 -> x1, local copies, waits for them, and re-layouts: none -> 14.1 us  [body(): normed.reshape(fr_local, band, width, chans) * norm_gain + norm_shift]
    all_to_all x1, blocking collectives: 49.4 us -> 57 us  [body(): lax.all_to_all(current, 'tm', split_axis=0, concat_axis=2, tiled=True)]
    convert_element_type x1, other arithmetic: 1.45 us -> 8.68 us  [body(): hidden = jax.nn.silu(normed).astype(jnp.bfloat16)]
    ppermute x0 -> x15, waiting for transfers between devices: none -> 4.97 us  [exchange_in_pairs(): outs.append(lax.ppermute(sent, axis, [(i, i ^ step) for i in range(size)]))]
  transfers between devices with their start and end apart: 2 -> 17, of which waited for: 2 -> 4; matrix products, arithmetic and copies ran while one was open for 1% -> 18% of each run, Pallas kernels for 0% -> 0%
where the time goes in v1:
time: 234 us; the launch traced here: 233 us
  local copies, waits for them, and re-layouts  95.9 us (41%)
  blocking collectives  60.7 us (26%)
  starting transfers between devices  37.9 us (16%)
  matrix products  14 us (6%)
  other arithmetic  13.4 us (6%)
  waiting for transfers between devices  10.6 us (5%)
    all_to_all x1, blocking collectives, body(): lax.all_to_all(current, 'tm', split_axis=0, concat_axis=2, tiled=True)  57 us
    another operation x17, local copies, waits for them, and re-layouts  51.6 us
    ppermute x15, starting transfers between devices, exchange_in_pairs(): outs.append(lax.ppermute(sent, axis, [(i, i ^ step) for i in range(size)]))  32.6 us
    unnamed x41, local copies, waits for them, and re-layouts  17.8 us
    reshape x1, local copies, waits for them, and re-layouts, body(): normed.reshape(fr_local, band, width, chans) * norm_gain + norm_shift  14.1 us
    convert_element_type x1, other arithmetic, body(): hidden = jax.nn.silu(normed).astype(jnp.bfloat16)  8.68 us
    dot_general x1, matrix products, body(): jnp.dot(patches, spatial_weight.reshape(9 * chans, chans), preferred_elem...  7.05 us
    dot_general x9, matrix products, temporal_layer(): jnp.einsum('trwc,cd->trwd', extended[start:start + own], kernels[tap_inde...  6.94 us
  transfers between devices with their start and end apart: 17, of which 4 were waited for; matrix products, arithmetic and copies ran while one was open for 18% of the time, Pallas kernels for 0%

profile of v1, /device:TPU:1, one launch (start us, length us, event | category | flops | bytes accessed | tf_op | source)
XLA Modules:
  0.0 233.0 jit_solution(14676388461508914094)
XLA Ops:
  1.2 4.0 %collective-permute-start = (bf16[2,1,480,128]{3,2,1,0:T(8,128)(2,1)S(1)}, bf16[2,1,480,128]{3,2,1,0:T(8,128)(2,1)S(1)}, u32[]{:S(2)}, u32[]{:S(2)}) collective-permute-start(bf16[2,1,480,128]{3,2,1,0:T(8,128)(2,1)S(1)} %get-tuple-element.25), channel_id=1, source_target_pairs={{0,1},{2,3},{4,5},{6,7},{8,9},{10,11},{12,13},{14,15},{16,17},{18,... | collective-permute-start | bytes 737288 | tf_op jit(solution)/shard_map/ppermute | solution.py:38
  9.8 3.8 %collective-permute-done.1 = bf16[2,1,480,128]{3,2,1,0:T(8,128)(2,1)S(1)} collective-permute-done((bf16[2,1,480,128]{3,2,1,0:T(8,128)(2,1)S(1)}, bf16[2,1,480,128]{3,2,1,0:T(8,128)(2,1)S(1)}, u32[]{:S(2)}, u32[]{:S(2)}) %collective-permute-start.1) | collective-permute-done | bytes 245792 | tf_op jit(solution)/shard_map/ppermute | solution.py:39
  19.7 7.1 %fusion.36 = (f32[2,32]{1,0:T(2,128)S(1)}, f32[2,32]{1,0:T(2,128)S(1)}, f32[2,8,480,32,4]{2,3,4,1,0:T(8,128)}) fusion(bf16[32,4,1152,1,1]{2,1,0,4,3:T(4,128)(2,1)S(1)} %bitcast.147, bf16[2,8,480,1152]{3,2,1,0:T(8,128)(2,1)S(1)} %slice_dynamic-update-slice_fusion), kind=kOutput, calls=%fused_computation.90 | convolution fusion | flops 2267873280 | bytes 21922304 | tf_op jit(solution)/shard_map/dot_general | solution.py:68
  26.8 3.8 %all-reduce.4 = (f32[2,32]{1,0:T(2,128)S(1)}, f32[2,32]{1,0:T(2,128)S(1)}) all-reduce(f32[2,32]{1,0:T(2,128)S(1)} %get-tuple-element.6, f32[2,32]{1,0:T(2,128)S(1)} %get-tuple-element.5), channel_id=1, replica_groups=mesh['tm'=16,'rows'=2] {'rows'}, use_global_device_ids=true, to_apply=%region_3.4 | all-reduce | flops 128 | bytes 1024 | tf_op jit(solution)/shard_map/psum | solution.py:75
  30.5 2.9 %subtract_multiply_fusion = f32[2,8,480,32,4]{2,3,4,1,0:T(8,128)S(1)} fusion(f32[2,8,480,32,4]{2,3,4,1,0:T(8,128)} %get-tuple-element.29, f32[2,32]{1,0:T(2,128)S(1)} %get-tuple-element.28, f32[2,32]{1,0:T(2,128)S(1)} %get-tuple-element.27), kind=kLoop, calls=%fused_computation.8 | loop fusion | flops 1966080 | bytes 7864832 | tf_op jit(solution)/shard_map/mul | solution.py:79
  33.4 4.4 %copy.9 = f32[2,8,480,32,4]{2,1,4,3,0:T(8,128)} copy(f32[2,8,480,32,4]{2,3,4,1,0:T(8,128)S(1)} %subtract_multiply_fusion) | data formatting | bytes 7864320 | tf_op jit(solution)/shard_map/mul | solution.py:79
  37.8 14.1 %reshape.86 = f32[2,8,16,30,128]{3,2,1,4,0:T(8,128)} reshape(f32[2,8,480,32,4]{2,1,4,3,0:T(8,128)} %copy.9) | data formatting | bytes 7864320 | tf_op jit(solution)/shard_map/reshape | solution.py:82
  51.9 8.7 %multiply_convert_fusion = bf16[2,8,16,30,128]{3,2,1,4,0:T(8,128)(2,1)S(1)} fusion(f32[2,8,16,30,128]{3,2,1,4,0:T(8,128)} %reshape.86, f32[128]{0:T(128)S(1)} %copy-done.8, f32[128]{0:T(128)S(1)} %copy-done.9), kind=kLoop, calls=%fused_computation.3 | loop fusion | flops 6881280 | bytes 5899264 | tf_op jit(solution)/shard_map/convert_element_type | solution.py:83
  60.6 21.4 %constant_dynamic-slice_fusion = (bf16[2,8,1,30,128]{3,2,1,4,0:T(2,128)(2,1)S(1)}, bf16[2,8,1,30,128]{3,2,1,4,0:T(2,128)(2,1)S(1)}, bf16[2,8,1,30,128]{3,2,1,4,0...) fusion(bf16[2,8,16,30,128]{3,2,1,4,0:T(8,128)(2,1)S(1)} %multip, ...), kind=kLoop, calls=%fused_computation.70 | loop fusion | bytes 3932224 | tf_op jit(solution)/shard_map/dynamic-slice.15
  83.6 2.2 copy.11
  85.9 3.0 %collective-permute-start.2 = (bf16[2,8,30,128]{3,1,2,0:T(8,128)(2,1)}, bf16[2,8,30,128]{3,1,2,0:T(8,128)(2,1)}, u32[]{:S(2)}, u32[]{:S(2)}) collective-permute-start(bf16[2,8,30,128]{3,1,2,0:T(8,128)(2,1)} %bitcast.6), channel_id=1, source_target_pairs={{0,2},{2,0},{4,6},{6,4},{8,10},{10,8},{12,14},{14,12},{16,18},{18,... | collective-permute-start | bytes 368648 | tf_op jit(solution)/shard_map/ppermute | solution.py:26
  92.3 2.2 copy.13
  101.3 2.2 copy.16
  103.6 2.2 copy.17
  110.3 2.2 copy.20
  125.1 2.3 collective-permute-start.9
  131.0 3.3 %collective-permute-start.11 = (bf16[2,8,30,128]{3,1,2,0:T(8,128)(2,1)S(1)}, bf16[2,8,30,128]{3,1,2,0:T(8,128)(2,1)S(1)}, u32[]{:S(2)}, u32[]{:S(2)}) collective-permute-start(bf16[2,8,30,128]{3,1,2,0:T(8,128)(2,1)S(1)} %bitcast.153), channel_id=1, source_target_pairs={{0,20},{2,22},{4,16},{6,18},{8,28},{10,30},{12,24},{14,26},{16,4},... | collective-permute-start | bytes 368648 | tf_op jit(solution)/shard_map/ppermute | solution.py:26
  136.7 3.3 %collective-permute-start.13 = (bf16[2,8,30,128]{3,1,2,0:T(8,128)(2,1)S(1)}, bf16[2,8,30,128]{3,1,2,0:T(8,128)(2,1)S(1)}, u32[]{:S(2)}, u32[]{:S(2)}) collective-permute-start(bf16[2,8,30,128]{3,1,2,0:T(8,128)(2,1)S(1)} %bitcast.151), channel_id=1, source_target_pairs={{0,24},{2,26},{4,28},{6,30},{8,16},{10,18},{12,20},{14,22},{16,8},... | collective-permute-start | bytes 368648 | tf_op jit(solution)/shard_map/ppermute | solution.py:26
  140.6 7.4 %collective-permute-start.14 = (bf16[2,8,30,128]{3,1,2,0:T(8,128)(2,1)S(1)}, bf16[2,8,30,128]{3,1,2,0:T(8,128)(2,1)S(1)}, u32[]{:S(2)}, u32[]{:S(2)}) collective-permute-start(bf16[2,8,30,128]{3,1,2,0:T(8,128)(2,1)S(1)} %bitcast.150), channel_id=1, source_target_pairs={{0,26},{2,24},{4,30},{6,28},{8,18},{10,16},{12,22},{14,20},{16,10}... | collective-permute-start | bytes 368648 | tf_op jit(solution)/shard_map/ppermute | solution.py:26
  148.7 2.6 %collective-permute-start.15 = (bf16[2,8,30,128]{3,1,2,0:T(8,128)(2,1)S(1)}, bf16[2,8,30,128]{3,1,2,0:T(8,128)(2,1)S(1)}, u32[]{:S(2)}, u32[]{:S(2)}) collective-permute-start(bf16[2,8,30,128]{3,1,2,0:T(8,128)(2,1)S(1)} %bitcast.149), channel_id=1, source_target_pairs={{0,28},{2,30},{4,24},{6,26},{8,20},{10,22},{12,16},{14,18},{16,12}... | collective-permute-start | bytes 368648 | tf_op jit(solution)/shard_map/ppermute | solution.py:26
  152.9 4.0 %collective-permute-start.16 = (bf16[2,8,30,128]{3,1,2,0:T(8,128)(2,1)S(1)}, bf16[2,8,30,128]{3,1,2,0:T(8,128)(2,1)S(1)}, u32[]{:S(2)}, u32[]{:S(2)}) collective-permute-start(bf16[2,8,30,128]{3,1,2,0:T(8,128)(2,1)S(1)} %bitcast.148), channel_id=1, source_target_pairs={{0,30},{2,28},{4,26},{6,24},{8,22},{10,20},{12,18},{14,16},{16,14}... | collective-permute-start | bytes 368648 | tf_op jit(solution)/shard_map/ppermute | solution.py:26
  157.5 4.0 %collective-permute-done.12 = bf16[2,8,30,128]{3,1,2,0:T(8,128)(2,1)S(1)} collective-permute-done((bf16[2,8,30,128]{3,1,2,0:T(8,128)(2,1)S(1)}, bf16[2,8,30,128]{3,1,2,0:T(8,128)(2,1)S(1)}, u32[]{:S(2)}, u32[]{:S(2)}) %collective-permute-start.12) | collective-permute-done | bytes 122912 | tf_op jit(solution)/shard_map/ppermute | solution.py:26
  164.9 2.5 %gather_fusion = bf16[16,2,8,30,128]{4,2,3,1,0:T(8,128)(2,1)S(1)} fusion(bf16[16,2,8,30,128]{4,2,3,1,0:T(8,128)(2,1)} %bitcast_dynamic-update-slice_fusion, s32[1024]{0:T(1024)S(1)} %pad_clamp_fusion), kind=kCustom, calls=%fused_computation | custom fusion | bytes 3932224 | tf_op jit(solution)/shard_map/gather | solution.py:27
  174.3 57.0 %all_to_all.18 = bf16[32,8,30,128]{3,1,2,0:T(8,128)(2,1)S(1)} all-to-all(bf16[32,8,30,128]{3,1,2,0:T(8,128)(2,1)S(1)} %add_convert_fusion), channel_id=1, replica_groups=mesh['tm'=16,'rows'=2] {'tm'}, dimensions={0} | all-to-all | bytes 3932160 | tf_op jit(solution)/shard_map/all_to_all | solution.py:89
  (98 shorter events, 61.9 us)
Async XLA Ops:
  0.0 13.6 %copy-start = (bf16[2,8,480,128]{3,2,1,0:T(8,128)(2,1)S(1)}, bf16[2,8,480,128]{3,2,1,0:T(8,128)(2,1)}, u32[]{:S(2)}) copy-start(bf16[2,8,480,128]{3,2,1,0:T(8,128)(2,1)} %param.5) | copy-start | bytes 5898244
  1.2 8.6 %collective-permute-start = (bf16[2,1,480,128]{3,2,1,0:T(8,128)(2,1)S(1)}, bf16[2,1,480,128]{3,2,1,0:T(8,128)(2,1)S(1)}, u32[]{:S(2)}, u32[]{:S(2)}) collective-permute-start(bf16[2,1,480,128]{3,2,1,0:T(8,128)(2,1)S(1)} %get-tuple-element.25), channel_id=1, source_target_pairs={{0,1},{2,3},{4,5},{6,7},{8,9},{10,11},{12,13},{14,15},{16,17},{18,... | collective-permute-start | bytes 737288 | tf_op jit(solution)/shard_map/ppermute | solution.py:38
  5.2 8.4 %collective-permute-start.1 = (bf16[2,1,480,128]{3,2,1,0:T(8,128)(2,1)S(1)}, bf16[2,1,480,128]{3,2,1,0:T(8,128)(2,1)S(1)}, u32[]{:S(2)}, u32[]{:S(2)}) collective-permute-start(bf16[2,1,480,128]{3,2,1,0:T(8,128)(2,1)S(1)} %get-tuple-element.26), channel_id=1, source_target_pairs={{1,0},{3,2},{5,4},{7,6},{9,8},{11,10},{13,12},{15,14},{17,16},{19,... | collective-permute-start | bytes 737288 | tf_op jit(solution)/shard_map/ppermute | solution.py:39
  37.8 14.1 %copy-start.8 = (f32[128]{0:T(128)S(1)}, f32[128]{0:T(128)}, u32[]{:S(2)}) copy-start(f32[128]{0:T(128)} %param.8) | copy-start | bytes 1540
  37.8 14.1 %copy-start.9 = (f32[128]{0:T(128)S(1)}, f32[128]{0:T(128)}, u32[]{:S(2)}) copy-start(f32[128]{0:T(128)} %param.7) | copy-start | bytes 1540
  85.9 33.5 %collective-permute-start.2 = (bf16[2,8,30,128]{3,1,2,0:T(8,128)(2,1)}, bf16[2,8,30,128]{3,1,2,0:T(8,128)(2,1)}, u32[]{:S(2)}, u32[]{:S(2)}) collective-permute-start(bf16[2,8,30,128]{3,1,2,0:T(8,128)(2,1)} %bitcast.6), channel_id=1, source_target_pairs={{0,2},{2,0},{4,6},{6,4},{8,10},{10,8},{12,14},{14,12},{16,18},{18,... | collective-permute-start | bytes 368648 | tf_op jit(solution)/shard_map/ppermute | solution.py:26
  91.1 32.1 %collective-permute-start.3 = (bf16[2,8,30,128]{3,1,2,0:T(8,128)(2,1)}, bf16[2,8,30,128]{3,1,2,0:T(8,128)(2,1)}, u32[]{:S(2)}, u32[]{:S(2)}) collective-permute-start(bf16[2,8,30,128]{3,1,2,0:T(8,128)(2,1)} %bitcast.8), channel_id=1, source_target_pairs={{0,4},{2,6},{4,0},{6,2},{8,12},{10,14},{12,8},{14,10},{16,20},{18,... | collective-permute-start | bytes 368648 | tf_op jit(solution)/shard_map/ppermute | solution.py:26
  94.6 30.5 %collective-permute-start.4 = (bf16[2,8,30,128]{3,1,2,0:T(8,128)(2,1)}, bf16[2,8,30,128]{3,1,2,0:T(8,128)(2,1)}, u32[]{:S(2)}, u32[]{:S(2)}) collective-permute-start(bf16[2,8,30,128]{3,1,2,0:T(8,128)(2,1)} %bitcast.10), channel_id=1, source_target_pairs={{0,6},{2,4},{4,2},{6,0},{8,14},{10,12},{12,10},{14,8},{16,22},{18,... | collective-permute-start | bytes 368648 | tf_op jit(solution)/shard_map/ppermute | solution.py:26
  97.2 31.7 %collective-permute-start.5 = (bf16[2,8,30,128]{3,1,2,0:T(8,128)(2,1)}, bf16[2,8,30,128]{3,1,2,0:T(8,128)(2,1)}, u32[]{:S(2)}, u32[]{:S(2)}) collective-permute-start(bf16[2,8,30,128]{3,1,2,0:T(8,128)(2,1)} %bitcast.12), channel_id=1, source_target_pairs={{0,8},{2,10},{4,12},{6,14},{8,0},{10,2},{12,4},{14,6},{16,24},{18,... | collective-permute-start | bytes 368648 | tf_op jit(solution)/shard_map/ppermute | solution.py:26
  100.8 30.2 %collective-permute-start.6 = (bf16[2,8,30,128]{3,1,2,0:T(8,128)(2,1)}, bf16[2,8,30,128]{3,1,2,0:T(8,128)(2,1)}, u32[]{:S(2)}, u32[]{:S(2)}) collective-permute-start(bf16[2,8,30,128]{3,1,2,0:T(8,128)(2,1)} %bitcast.14), channel_id=1, source_target_pairs={{0,10},{2,8},{4,14},{6,12},{8,2},{10,0},{12,6},{14,4},{16,26},{18,... | collective-permute-start | bytes 368648 | tf_op jit(solution)/shard_map/ppermute | solution.py:26
  117.1 8.0 %copy-start.5 = (bf16[2,8,1,30,128]{4,1,3,0,2:T(8,128)(2,1)S(1)}, bf16[2,8,1,30,128]{4,1,3,0,2:T(8,128)(2,1)}, u32[]{:S(2)}) copy-start(bf16[2,8,1,30,128]{4,1,3,0,2:T(8,128)(2,1)} %copy.18) | copy-start | bytes 368644
  117.1 11.9 %copy-start.4 = (bf16[2,8,1,30,128]{4,1,3,0,2:T(8,128)(2,1)S(1)}, bf16[2,8,1,30,128]{4,1,3,0,2:T(8,128)(2,1)}, u32[]{:S(2)}) copy-start(bf16[2,8,1,30,128]{4,1,3,0,2:T(8,128)(2,1)} %copy.19) | copy-start | bytes 368644
  117.1 13.9 %copy-start.3 = (bf16[2,8,1,30,128]{4,1,3,0,2:T(8,128)(2,1)S(1)}, bf16[2,8,1,30,128]{4,1,3,0,2:T(8,128)(2,1)}, u32[]{:S(2)}) copy-start(bf16[2,8,1,30,128]{4,1,3,0,2:T(8,128)(2,1)} %copy.20) | copy-start | bytes 368644
  117.1 18.7 %copy-start.2 = (bf16[2,8,1,30,128]{4,1,3,0,2:T(8,128)(2,1)S(1)}, bf16[2,8,1,30,128]{4,1,3,0,2:T(8,128)(2,1)}, u32[]{:S(2)}) copy-start(bf16[2,8,1,30,128]{4,1,3,0,2:T(8,128)(2,1)} %copy.21) | copy-start | bytes 368644
  119.4 16.4 %collective-permute-start.7 = (bf16[2,8,30,128]{3,1,2,0:T(8,128)(2,1)S(1)}, bf16[2,8,30,128]{3,1,2,0:T(8,128)(2,1)S(1)}, u32[]{:S(2)}, u32[]{:S(2)}) collective-permute-start(bf16[2,8,30,128]{3,1,2,0:T(8,128)(2,1)S(1)} %bitcast.157), channel_id=1, source_target_pairs={{0,12},{2,14},{4,8},{6,10},{8,4},{10,6},{12,0},{14,2},{16,28},{18,... | collective-permute-start | bytes 368648 | tf_op jit(solution)/shard_map/ppermute | solution.py:26
  123.2 13.5 %collective-permute-start.8 = (bf16[2,8,30,128]{3,1,2,0:T(8,128)(2,1)S(1)}, bf16[2,8,30,128]{3,1,2,0:T(8,128)(2,1)S(1)}, u32[]{:S(2)}, u32[]{:S(2)}) collective-permute-start(bf16[2,8,30,128]{3,1,2,0:T(8,128)(2,1)S(1)} %bitcast.156), channel_id=1, source_target_pairs={{0,14},{2,12},{4,10},{6,8},{8,6},{10,4},{12,2},{14,0},{16,30},{18,... | collective-permute-start | bytes 368648 | tf_op jit(solution)/shard_map/ppermute | solution.py:26
  125.1 15.5 %collective-permute-start.9 = (bf16[2,8,30,128]{3,1,2,0:T(8,128)(2,1)S(1)}, bf16[2,8,30,128]{3,1,2,0:T(8,128)(2,1)S(1)}, u32[]{:S(2)}, u32[]{:S(2)}) collective-permute-start(bf16[2,8,30,128]{3,1,2,0:T(8,128)(2,1)S(1)} %bitcast.155), channel_id=1, source_target_pairs={{0,16},{2,18},{4,20},{6,22},{8,24},{10,26},{12,28},{14,30},{16,0},... | collective-permute-start | bytes 368648 | tf_op jit(solution)/shard_map/ppermute | solution.py:26
  129.0 19.7 %collective-permute-start.10 = (bf16[2,8,30,128]{3,1,2,0:T(8,128)(2,1)S(1)}, bf16[2,8,30,128]{3,1,2,0:T(8,128)(2,1)S(1)}, u32[]{:S(2)}, u32[]{:S(2)}) collective-permute-start(bf16[2,8,30,128]{3,1,2,0:T(8,128)(2,1)S(1)} %bitcast.154), channel_id=1, source_target_pairs={{0,18},{2,16},{4,22},{6,20},{8,26},{10,24},{12,30},{14,28},{16,2},... | collective-permute-start | bytes 368648 | tf_op jit(solution)/shard_map/ppermute | solution.py:26
  131.0 21.9 %collective-permute-start.11 = (bf16[2,8,30,128]{3,1,2,0:T(8,128)(2,1)S(1)}, bf16[2,8,30,128]{3,1,2,0:T(8,128)(2,1)S(1)}, u32[]{:S(2)}, u32[]{:S(2)}) collective-permute-start(bf16[2,8,30,128]{3,1,2,0:T(8,128)(2,1)S(1)} %bitcast.153), channel_id=1, source_target_pairs={{0,20},{2,22},{4,16},{6,18},{8,28},{10,30},{12,24},{14,26},{16,4},... | collective-permute-start | bytes 368648 | tf_op jit(solution)/shard_map/ppermute | solution.py:26
  135.8 25.8 %collective-permute-start.12 = (bf16[2,8,30,128]{3,1,2,0:T(8,128)(2,1)S(1)}, bf16[2,8,30,128]{3,1,2,0:T(8,128)(2,1)S(1)}, u32[]{:S(2)}, u32[]{:S(2)}) collective-permute-start(bf16[2,8,30,128]{3,1,2,0:T(8,128)(2,1)S(1)} %bitcast.152), channel_id=1, source_target_pairs={{0,22},{2,20},{4,18},{6,16},{8,30},{10,28},{12,26},{14,24},{16,6},... | collective-permute-start | bytes 368648 | tf_op jit(solution)/shard_map/ppermute | solution.py:26
  136.7 25.5 %collective-permute-start.13 = (bf16[2,8,30,128]{3,1,2,0:T(8,128)(2,1)S(1)}, bf16[2,8,30,128]{3,1,2,0:T(8,128)(2,1)S(1)}, u32[]{:S(2)}, u32[]{:S(2)}) collective-permute-start(bf16[2,8,30,128]{3,1,2,0:T(8,128)(2,1)S(1)} %bitcast.151), channel_id=1, source_target_pairs={{0,24},{2,26},{4,28},{6,30},{8,16},{10,18},{12,20},{14,22},{16,8},... | collective-permute-start | bytes 368648 | tf_op jit(solution)/shard_map/ppermute | solution.py:26
  140.6 22.2 %collective-permute-start.14 = (bf16[2,8,30,128]{3,1,2,0:T(8,128)(2,1)S(1)}, bf16[2,8,30,128]{3,1,2,0:T(8,128)(2,1)S(1)}, u32[]{:S(2)}, u32[]{:S(2)}) collective-permute-start(bf16[2,8,30,128]{3,1,2,0:T(8,128)(2,1)S(1)} %bitcast.150), channel_id=1, source_target_pairs={{0,26},{2,24},{4,30},{6,28},{8,18},{10,16},{12,22},{14,20},{16,10}... | collective-permute-start | bytes 368648 | tf_op jit(solution)/shard_map/ppermute | solution.py:26
  148.7 14.8 %collective-permute-start.15 = (bf16[2,8,30,128]{3,1,2,0:T(8,128)(2,1)S(1)}, bf16[2,8,30,128]{3,1,2,0:T(8,128)(2,1)S(1)}, u32[]{:S(2)}, u32[]{:S(2)}) collective-permute-start(bf16[2,8,30,128]{3,1,2,0:T(8,128)(2,1)S(1)} %bitcast.149), channel_id=1, source_target_pairs={{0,28},{2,30},{4,24},{6,26},{8,20},{10,22},{12,16},{14,18},{16,12}... | collective-permute-start | bytes 368648 | tf_op jit(solution)/shard_map/ppermute | solution.py:26
  152.9 11.3 %collective-permute-start.16 = (bf16[2,8,30,128]{3,1,2,0:T(8,128)(2,1)S(1)}, bf16[2,8,30,128]{3,1,2,0:T(8,128)(2,1)S(1)}, u32[]{:S(2)}, u32[]{:S(2)}) collective-permute-start(bf16[2,8,30,128]{3,1,2,0:T(8,128)(2,1)S(1)} %bitcast.148), channel_id=1, source_target_pairs={{0,30},{2,28},{4,26},{6,24},{8,22},{10,20},{12,18},{14,16},{16,14}... | collective-permute-start | bytes 368648 | tf_op jit(solution)/shard_map/ppermute | solution.py:26
  (3 other events, 12.9 us)
